TPU v7x, 256 devices: a whole 4x4x8 slice. The times are simulated.
256 devices in a mesh: grp: 4 (over y), shard: 64 (over z, x, core).
Axes of the slice: x: 4, y: 4, z: 8, core: 2. Of those that a mesh axis runs over, the one named last changes fastest.
Arguments:
- query_rows: bfloat16 [65536, 1024], P(('grp', 'shard')), may hold values from -6 to 6
- key_rows: bfloat16 [65536, 1024], P(('grp', 'shard')), may hold values from -6 to 6
- value_rows: bfloat16 [65536, 1024], P(('grp', 'shard')), may hold values from -6 to 6
- grad_out: bfloat16 [65536, 1024], P(('grp', 'shard')), may hold values from -6 to 6
Outputs:
- attended: bfloat16 [65536, 1024], P(('grp', 'shard'))
- grad_query: bfloat16 [65536, 1024], P(('grp', 'shard'))
- grad_key: bfloat16 [65536, 1024], P(('grp', 'shard'))
- grad_value: bfloat16 [65536, 1024], P(('grp', 'shard'))
All inputs are finite; a program needn't handle non-finite values.
Results may differ from a plain program's by a relative error of at most 0.012.
Values may be sent and summed in bfloat16 or wider, within the bound.
A program may use at most 256 MiB of HBM per device.

v0:
```python
import jax
import jax.numpy as jnp
from jax import lax
from jax.sharding import PartitionSpec as P

HD = 128


def entering(array, axis, join, neutral, backward):
    count = lax.axis_size(axis)
    place = lax.axis_index(axis)
    ahead = count - 1 - place if backward else place
    gathered = lax.all_gather(array.astype(jnp.bfloat16), axis)
    state = jnp.zeros_like(array) + jnp.asarray(neutral, array.dtype)

    def one(step, state):
        source = count - 1 - step if backward else step
        return join(state, lax.dynamic_index_in_dim(gathered, source, 0, False).astype(array.dtype))

    return lax.fori_loop(0, ahead, one, state)


def add_states(earlier, later_part):
    return earlier + later_part


def prefix_states(local_state, backward):
    empty_state = jnp.zeros_like(local_state)
    inside = entering(local_state, "shard", add_states, empty_state, backward)
    group_sum = lax.psum(local_state, "shard")
    outside = entering(group_sum, "grp", add_states, empty_state, backward)
    return inside + outside


def body(query_rows, key_rows, value_rows, grad_out):
    row_count = query_rows.shape[0]
    head_size = HD
    head_count = query_rows.shape[1] // head_size
    query_heads = query_rows.reshape(row_count, head_count, head_size)
    key_heads = key_rows.reshape(row_count, head_count, head_size)
    value_heads = value_rows.reshape(row_count, head_count, head_size)
    rows_at = lax.broadcasted_iota(jnp.int32, (row_count, row_count), 0)
    cols_at = lax.broadcasted_iota(jnp.int32, (row_count, row_count), 1)
    causal = (rows_at >= cols_at)[None]
    block_state = jnp.einsum(
        "thd,the->hde", key_heads, value_heads, preferred_element_type=jnp.float32
    )
    earlier = prefix_states(block_state, False)
    scores = jnp.einsum("thd,shd->hts", query_heads, key_heads, preferred_element_type=jnp.float32)
    local_scores = jnp.where(causal, scores, 0.0).astype(jnp.bfloat16)
    local_mixed = jnp.einsum(
        "hts,she->the", local_scores, value_heads, preferred_element_type=jnp.float32
    )
    earlier_rounded = earlier.astype(jnp.bfloat16)
    mixed_rows = local_mixed + jnp.einsum(
        "thd,hde->the", query_heads, earlier_rounded, preferred_element_type=jnp.float32
    )
    inv_rms = lax.rsqrt(jnp.mean(mixed_rows * mixed_rows, axis=-1, keepdims=True) + 1.0)
    normed = mixed_rows * inv_rms
    attended = normed.astype(jnp.bfloat16).reshape(row_count, head_count * head_size)
    grad_heads = grad_out.reshape(row_count, head_count, head_size).astype(jnp.float32)
    grad_mixed = (
        (grad_heads - normed * jnp.mean(grad_heads * normed, axis=-1, keepdims=True)) * inv_rms
    ).astype(jnp.bfloat16)
    block_reverse = jnp.einsum(
        "thd,the->hde", query_heads, grad_mixed, preferred_element_type=jnp.float32
    )
    later_sum = prefix_states(block_reverse, True)
    grad_raw = jnp.einsum(
        "the,she->hts", grad_mixed, value_heads, preferred_element_type=jnp.float32
    )
    grad_scores = jnp.where(causal, grad_raw, 0.0).astype(jnp.bfloat16)
    grad_query = jnp.einsum(
        "hts,shd->thd", grad_scores, key_heads, preferred_element_type=jnp.float32
    )
    grad_query = grad_query + jnp.einsum(
        "the,hde->thd", grad_mixed, earlier_rounded, preferred_element_type=jnp.float32
    )
    key_local = jnp.einsum(
        "hts,thd->shd", grad_scores, query_heads, preferred_element_type=jnp.float32
    )
    value_local = jnp.einsum(
        "hts,the->she", local_scores, grad_mixed, preferred_element_type=jnp.float32
    )
    later_rounded = later_sum.astype(jnp.bfloat16)
    grad_key = key_local + jnp.einsum(
        "she,hde->shd", value_heads, later_rounded, preferred_element_type=jnp.float32
    )
    grad_value = value_local + jnp.einsum(
        "shd,hde->she", key_heads, later_rounded, preferred_element_type=jnp.float32
    )
    flat_width = head_count * head_size
    return (
        attended,
        grad_query.astype(jnp.bfloat16).reshape(row_count, flat_width),
        grad_key.astype(jnp.bfloat16).reshape(row_count, flat_width),
        grad_value.astype(jnp.bfloat16).reshape(row_count, flat_width),
    )


def solution(mesh):
    in_specs = (
        P(("grp", "shard"), None),
        P(("grp", "shard"), None),
        P(("grp", "shard"), None),
        P(("grp", "shard"), None),
    )
    out_specs = (
        P(("grp", "shard"), None),
        P(("grp", "shard"), None),
        P(("grp", "shard"), None),
        P(("grp", "shard"), None),
    )
    return jax.shard_map(body, mesh=mesh, in_specs=in_specs, out_specs=out_specs, check_vma=False)
```

profile of v0, /device:TPU:1, one launch (start us, length us, event | category | flops | bytes accessed | tf_op | source)
XLA Modules:
  0.0 917.8 jit_solution(16972495328482349829)
XLA Ops:
  7.2 1.2 copy.61
  9.8 252.9 %all-reduce.2 = bf16[8,128,128]{2,1,0:T(8,128)(2,1)} all-reduce(f32[8,128,128]{2,1,0:T(8,128)S(1)} %get-tuple-element.217), channel_id=1, replica_groups=mesh['grp'=4,'shard'=64] {'shard'}, use_global_device_ids=true, to_apply=%region_2.3 | all-reduce | flops 131072 | bytes 786432 | tf_op jit(solution)/shard_map/psum | solution.py:30
  263.5 1.2 copy.38
  266.3 1.5 convolution_bitcast_fusion.5
  267.7 19.5 %all-gather.11.cloned.1.call-done = bf16[32,128,128]{2,1,0:T(8,128)(2,1)} async-done(((bf16[8,128,128]{2,1,0:T(8,128)(2,1)}), bf16[32,128,128]{2,1,0:T(8,128)(2,1)}) %all-gather.11.cloned.1.call-update) | async-done | bytes 1048592 | tf_op jit(solution)/shard_map/all_gather | solution.py:13
  287.3 105.4 %all-gather.9.cloned.1.call-done = bf16[512,128,128]{2,1,0:T(8,128)(2,1)} async-done(((bf16[8,128,128]{2,1,0:T(8,128)(2,1)}), bf16[512,128,128]{2,1,0:T(8,128)(2,1)}) %all-gather.9.cloned.1.call-update) | async-done | bytes 16777232 | tf_op jit(solution)/shard_map/all_gather | solution.py:13
  392.7 1.1 while.44
  393.9 1.6 multiply_reduce_fusion.1
  397.0 313.1 %all-reduce.3 = bf16[8,128,128]{1,2,0:T(8,128)(2,1)S(1)} all-reduce(f32[8,128,128]{1,2,0:T(8,128)S(1)} %get-tuple-element.221), channel_id=1, replica_groups=mesh['grp'=4,'shard'=64] {'shard'}, use_global_device_ids=true, to_apply=%region_9.10 | all-reduce | flops 131072 | bytes 786432 | tf_op jit(solution)/shard_map/psum | solution.py:30
  712.9 1.1 fusion.3
  714.0 2.0 copy.51
  717.0 1.3 fusion.29
  718.7 15.7 %all-gather.15.cloned.1.call-done = bf16[32,128,128]{2,1,0:T(8,128)(2,1)} async-done(((bf16[8,128,128]{2,1,0:T(8,128)(2,1)}), bf16[32,128,128]{2,1,0:T(8,128)(2,1)}) %all-gather.15.cloned.1.call-update) | async-done | bytes 1048592 | tf_op jit(solution)/shard_map/all_gather | solution.py:13
  734.4 3.3 while.47
  734.4 1.1 convert_add_fusion.11
  735.5 1.1 convert_add_fusion.11
  736.6 1.1 convert_add_fusion.11
  737.7 101.4 %all-gather.13.cloned.1.call-done = bf16[512,128,128]{2,1,0:T(8,128)(2,1)} async-done(((bf16[8,128,128]{2,1,0:T(8,128)(2,1)}), bf16[512,128,128]{2,1,0:T(8,128)(2,1)}) %all-gather.13.cloned.1.call-update) | async-done | bytes 16777232 | tf_op jit(solution)/shard_map/all_gather | solution.py:13
  839.1 68.0 %while.46 = (s32[]{:T(128)}, f32[8,128,128]{2,1,0:T(8,128)S(1)}, s32[]{:T(128)}, bf16[64,8,128,128]{3,2,1,0:T(8,128)(2,1)}, s32[]{:T(128)}, /*index=5*/s32[]{:T(128)}, s32[]{:T(128)}, s32[]{:T(128)}) while((s32[]{:T(128)}, f32[8,128,128]{2,1,0:T(8,128)S(1)}, s32[]{:T(128)}, bf16[64,8,128,128]{3,2,1,0:T(8,128)(2,1)}, s32[]{:T(128)}, ...), condition=%wide.region_8.9_spmd, body=%wide.region_7.8_spmd.sunk | while | flops 262150 | bytes 1310855 | solution.py:20
  840.2 1.1 convert_add_fusion.10
  841.3 1.1 convert_add_fusion.10
  842.4 1.1 convert_add_fusion.10
  843.5 1.1 convert_add_fusion.10
  844.6 1.1 convert_add_fusion.10
  845.7 1.1 convert_add_fusion.10
  846.8 1.1 convert_add_fusion.10
  851.2 1.1 convert_add_fusion.10
  852.3 1.1 convert_add_fusion.10
  853.4 1.1 convert_add_fusion.10
  854.5 1.1 convert_add_fusion.10
  855.6 1.1 convert_add_fusion.10
  856.7 1.1 convert_add_fusion.10
  861.1 1.1 convert_add_fusion.10
  862.2 1.1 convert_add_fusion.10
  863.3 1.1 convert_add_fusion.10
  864.4 1.1 convert_add_fusion.10
  865.5 1.1 convert_add_fusion.10
  866.6 1.1 convert_add_fusion.10
  867.6 1.1 convert_add_fusion.10
  872.0 1.1 convert_add_fusion.10
  873.1 1.1 convert_add_fusion.10
  874.2 1.1 convert_add_fusion.10
  875.3 1.1 convert_add_fusion.10
  876.4 1.1 convert_add_fusion.10
  877.5 1.1 convert_add_fusion.10
  881.9 1.1 convert_add_fusion.10
  883.0 1.1 convert_add_fusion.10
  907.2 1.7 fusion.5
  (90 shorter events, 49.2 us)
Async XLA Ops:
  7.2 257.7 %copy-start = (bf16[256,1024]{1,0:T(8,128)(2,1)S(1)}, bf16[256,1024]{1,0:T(8,128)(2,1)}, u32[]{:S(2)}) copy-start(bf16[256,1024]{1,0:T(8,128)(2,1)} %param.12) | copy-start | bytes 1572868
  7.2 1.6 copy-start.3
  7.2 280.0 %all-gather.11.cloned.1.call-start = ((), (), s32[]{:S(2)}) async-start(), calls=%async_computation.1 | async-start | bytes 1310720 | tf_op jit(solution)/shard_map/all_gather | solution.py:13
  8.8 256.0 %copy-start.1 = (bf16[256,8,128]{0,2,1:T(8,128)(2,1)}, bf16[256,8,128]{0,2,1:T(8,128)(2,1)S(1)}, u32[]{:S(2)}) copy-start(bf16[256,8,128]{0,2,1:T(8,128)(2,1)S(1)} %copy.34) | copy-start | bytes 1572868
  8.8 256.0 %copy-start.9 = (bf16[256,1024]{1,0:T(8,128)(2,1)S(1)}, bf16[256,1024]{1,0:T(8,128)(2,1)}, u32[]{:S(2)}) copy-start(bf16[256,1024]{1,0:T(8,128)(2,1)} %param.13) | copy-start | bytes 1572868
  262.7 129.9 %all-gather.9.cloned.1.call-start = ((), (), s32[]{:S(2)}) async-start(), calls=%async_computation | async-start | bytes 17039360 | tf_op jit(solution)/shard_map/all_gather | solution.py:13
  263.5 470.9 %all-gather.15.cloned.1.call-start = ((), (), s32[]{:S(2)}) async-start(), calls=%async_computation.3 | async-start | bytes 1310720 | tf_op jit(solution)/shard_map/all_gather | solution.py:13
  265.3 1.0 copy-start.5
  396.7 315.2 %copy-start.4 = (bf16[256,1024]{1,0:T(8,128)(2,1)S(1)}, bf16[256,1024]{1,0:T(8,128)(2,1)}, u32[]{:S(2)}) copy-start(bf16[256,1024]{1,0:T(8,128)(2,1)} %param.14) | copy-start | bytes 1572868
  710.0 2.3 copy-start.2
  710.9 128.1 %all-gather.13.cloned.1.call-start = ((), (), s32[]{:S(2)}) async-start(), calls=%async_computation.2 | async-start | bytes 17039360 | tf_op jit(solution)/shard_map/all_gather | solution.py:13
  712.4 1.6 copy-start.7
  712.9 3.1 copy-start.10
  712.9 4.1 copy-start.6
  717.0 1.3 copy-start.8
Sparse Core Ops, SparseCore 0:
  262.9 24.3 all-gather.10
  290.6 102.0 all-gather.8
  711.0 23.2 all-gather.14
  737.0 102.0 all-gather.12
where the time goes:
time: 920 us; the launch traced here: 918 us
  blocking collectives  566 us (62%)
  waiting for transfers between devices  243 us (26%)
  other arithmetic  71.9 us (8%)
  between operations  14 us (2%)
  local copies, waits for them, and re-layouts  10.7 us (1%)
  matrix products  10.5 us (1%)
    psum x2, blocking collectives, prefix_states(): group_sum = lax.psum(local_state, 'shard')  566 us
    all_gather x4, waiting for transfers between devices, entering(): gathered = lax.all_gather(array.astype(jnp.bfloat16), axis)  242 us
    add x66, other arithmetic, add_states(): return earlier + later_part  70.6 us
  transfers between devices with their start and end apart: 4, of which 4 were waited for; matrix products, arithmetic and copies ran while one was open for 2% of the time, Pallas kernels for 0%

commit v1 on v0

v1 whole, which is shorter than its diff:
```python
import functools

import jax
import jax.numpy as jnp
from jax import lax
from jax.experimental import pallas as pl
from jax.experimental.pallas import tpu as pltpu
from jax.sharding import PartitionSpec as P

HD = 128
ROW = 8
MESH = pl.DeviceIdType.MESH
F32 = jnp.float32
BF16 = jnp.bfloat16


def dot(a, b, ca, cb):
    return lax.dot_general(a, b, (((ca,), (cb,)), ((), ())), preferred_element_type=F32)


def head(ref, h):
    if isinstance(h, int):
        return ref.at[:, h * HD:(h + 1) * HD]
    return ref.at[:, pl.ds(pl.multiple_of(h * HD, HD), HD)]


def scan_kernel(ny, nz, q_ref, k_ref, v_ref, g_ref, att_ref, gq_ref, kl_ref, vl_ref, later_ref,
                ls, lm, gm, s1, r1, ry, ab, rz, s4, r4,
                ss1, rs1, ssy, rsy, ssz, rsz, ss4, rs4):
    y = lax.axis_index("grp")
    shard = lax.axis_index("shard")
    z = shard // ROW
    j = lax.rem(shard, ROW)
    tok = q_ref.shape[0]
    order = (4, 3, 5, 2, 6, 1, 7)

    def in_row(d):
        return lax.rem(j + d, ROW)

    barrier = pltpu.get_barrier_semaphore()
    for d in range(1, ROW):
        pl.semaphore_signal(barrier, inc=1, device_id=(y, z * ROW + in_row(d)), device_id_type=MESH)
    for d in range(1, ny):
        pl.semaphore_signal(barrier, inc=1, device_id=(lax.rem(y + d, ny), shard), device_id_type=MESH)
    for d in range(1, nz):
        pl.semaphore_signal(barrier, inc=1, device_id=(y, lax.rem(z + d, nz) * ROW + j), device_id_type=MESH)

    def to_owner(i, d):
        return pltpu.make_async_remote_copy(
            src_ref=s1.at[i, d], dst_ref=r1.at[i, j], send_sem=ss1.at[i, d], recv_sem=rs1.at[i, d],
            device_id=(y, z * ROW + in_row(d)), device_id_type=MESH)

    def along_y(i, d):
        return pltpu.make_async_remote_copy(
            src_ref=ry.at[i, y], dst_ref=ry.at[i, y], send_sem=ssy.at[i, d], recv_sem=rsy.at[i, d],
            device_id=(lax.rem(y + d, ny), shard), device_id_type=MESH)

    def along_z(i, d):
        there = lax.rem(z + d, nz)
        beyond = (there > z) if i == 0 else (there < z)
        return pltpu.make_async_remote_copy(
            src_ref=ab.at[i, 1 - beyond.astype(jnp.int32)], dst_ref=rz.at[i, d - 1],
            send_sem=ssz.at[i, d], recv_sem=rsz.at[i, d],
            device_id=(y, there * ROW + j), device_id_type=MESH)

    def from_owner(i, d):
        return pltpu.make_async_remote_copy(
            src_ref=s4.at[i, in_row(d)], dst_ref=r4.at[i, j], send_sem=ss4.at[i, d], recv_sem=rs4.at[i, d],
            device_id=(y, z * ROW + in_row(d)), device_id_type=MESH)

    def causal():
        rows_at = lax.broadcasted_iota(jnp.int32, (tok, tok), 0)
        cols_at = lax.broadcasted_iota(jnp.int32, (tok, tok), 1)
        return rows_at >= cols_at

    def middle(i, fill_a, fill_b):
        fill_a()
        for d in order:
            to_owner(i, d).wait_recv()
        total = r1[i, 0].astype(F32)
        for n in range(1, ROW):
            total = total + r1[i, n].astype(F32)
        ry[i, y] = total.astype(BF16)
        for d in range(1, ny):
            along_y(i, d).start()
        for d in range(1, ny):
            along_y(i, d).wait_recv()
        before = jnp.zeros((HD, HD), F32)
        for n in range(ny):
            inside = (n < y) if i == 0 else (n > y)
            before = before + ry[i, n].astype(F32) * inside.astype(F32)
        upto = before + ry[i, y].astype(F32)
        ab[i, 0] = upto.astype(BF16)
        ab[i, 1] = before.astype(BF16)
        for d in (4, 3, 5, 2, 6, 1, 7):
            if d < nz:
                along_z(i, d).start()
        fill_b()
        base = before
        for d in range(1, nz):
            along_z(i, d).wait_recv()
            base = base + rz[i, d - 1].astype(F32)
        for n in (range(ROW) if i == 0 else range(ROW - 1, -1, -1)):
            s4[i, n] = base.astype(BF16)
            base = base + r1[i, n].astype(F32)
        for d in order:
            from_owner(i, d).start()
        r4[i, j] = s4[i, j]

    for d in order:
        h = in_row(d)
        s1[0, d] = dot(head(k_ref, h)[...], head(v_ref, h)[...], 0, 0).astype(BF16)
    pl.semaphore_wait(barrier, ROW - 1 + ny - 1 + nz - 1)
    for d in order:
        to_owner(0, d).start()
    r1[0, j] = dot(head(k_ref, j)[...], head(v_ref, j)[...], 0, 0).astype(BF16)

    def forward_local():
        def one(h, carry):
            scores = dot(head(q_ref, h)[...], head(k_ref, h)[...], 1, 1)
            scores = jnp.where(causal(), scores, 0.0).astype(BF16)
            ls[h] = scores
            lm[h] = dot(scores, head(v_ref, h)[...], 1, 0)
            return carry
        lax.fori_loop(0, ROW, one, 0)

    middle(0, forward_local, lambda: None)

    for d in (0, 1, 7, 2, 6, 3, 5, 4):
        h = in_row(d)
        if d:
            from_owner(0, ROW - d).wait_recv()
        q = head(q_ref, h)[...]
        mixed = lm[h] + dot(q, r4[0, h], 1, 0)
        inv_rms = lax.rsqrt(jnp.mean(mixed * mixed, axis=-1, keepdims=True) + 1.0)
        normed = mixed * inv_rms
        head(att_ref, h)[...] = normed.astype(BF16)
        grad = head(g_ref, h)[...].astype(F32)
        grad_mixed = ((grad - normed * jnp.mean(grad * normed, axis=-1, keepdims=True)) * inv_rms).astype(BF16)
        gm[h] = grad_mixed
        reverse = dot(q, grad_mixed, 0, 0).astype(BF16)
        if d:
            s1[1, d] = reverse
            to_owner(1, d).start()
        else:
            r1[1, j] = reverse

    def backward_local(first, last):
        def one(h, carry):
            grad_mixed = gm[h]
            k = head(k_ref, h)[...]
            scores = dot(grad_mixed, head(v_ref, h)[...], 1, 1)
            scores = jnp.where(causal(), scores, 0.0).astype(BF16)
            query = dot(scores, k, 1, 0) + dot(grad_mixed, r4[0, h], 1, 1)
            head(gq_ref, h)[...] = query.astype(BF16)
            head(kl_ref, h)[...] = dot(scores, head(q_ref, h)[...], 0, 0)
            head(vl_ref, h)[...] = dot(ls[h], grad_mixed, 0, 0)
            return carry
        lax.fori_loop(first, last, one, 0)

    middle(1, lambda: backward_local(0, 4), lambda: backward_local(4, 8))

    for d in order:
        from_owner(1, d).wait_recv()
    later_ref[...] = r4[1]

    for i in range(2):
        for d in order:
            to_owner(i, d).wait_send()
            from_owner(i, d).wait_send()
        for d in range(1, ny):
            along_y(i, d).wait_send()
        for d in range(1, nz):
            along_z(i, d).wait_send()


def final_kernel(k_ref, v_ref, later_ref, kl_ref, vl_ref, a_ref, q_ref, att_ref, gq_ref, gk_ref, gv_ref):
    att_ref[...] = a_ref[...]
    gq_ref[...] = q_ref[...]
    for h in range(ROW):
        later = later_ref[h]
        head(gk_ref, h)[...] = (head(kl_ref, h)[...] + dot(head(v_ref, h)[...], later, 1, 1)).astype(BF16)
        head(gv_ref, h)[...] = (head(vl_ref, h)[...] + dot(head(k_ref, h)[...], later, 1, 0)).astype(BF16)


def body(ny, nz, q, k, v, g):
    tok, width = q.shape
    vmem = pl.BlockSpec(memory_space=pltpu.VMEM)
    rows = jax.ShapeDtypeStruct((tok, width), BF16)
    rows_f32 = jax.ShapeDtypeStruct((tok, width), F32)
    dma = pltpu.SemaphoreType.DMA
    state = lambda n: pltpu.VMEM((2, n, HD, HD), BF16)
    att, gq, kl, vl, later = pl.pallas_call(
        functools.partial(scan_kernel, ny, nz),
        out_shape=(rows, rows, rows_f32, rows_f32, jax.ShapeDtypeStruct((ROW, HD, HD), BF16)),
        in_specs=[vmem] * 4,
        out_specs=(vmem,) * 5,
        scratch_shapes=[
            pltpu.VMEM((ROW, tok, tok), BF16),
            pltpu.VMEM((ROW, tok, HD), F32),
            pltpu.VMEM((ROW, tok, HD), BF16),
            state(ROW), state(ROW), state(ny), state(2), state(nz), state(ROW), state(ROW),
            dma((2, ROW)), dma((2, ROW)), dma((2, ny)), dma((2, ny)),
            dma((2, nz)), dma((2, nz)), dma((2, ROW)), dma((2, ROW)),
        ],
        compiler_params=pltpu.CompilerParams(collective_id=0, has_side_effects=True),
        name="scan",
    )(q, k, v, g)
    tile = tok // 2
    narrow = pl.BlockSpec((tile, width), lambda i: (i, 0))
    whole = pl.BlockSpec((ROW, HD, HD), lambda i: (0, 0, 0))
    return pl.pallas_call(
        final_kernel,
        grid=(2,),
        out_shape=(rows,) * 4,
        in_specs=[narrow, narrow, whole, narrow, narrow, narrow, narrow],
        out_specs=(narrow,) * 4,
        name="final",
    )(k, v, later, kl, vl, att, gq)


def solution(mesh):
    ny = mesh.shape["grp"]
    nz = mesh.shape["shard"] // ROW
    spec = P(("grp", "shard"), None)
    return jax.shard_map(functools.partial(body, ny, nz), mesh=mesh, in_specs=(spec,) * 4,
                         out_specs=(spec,) * 4, check_vma=False)
```

time: 920 us -> 61.8 us (0.07)
  blocking collectives: 566 us -> 0 us
  waiting for transfers between devices: 243 us -> 0 us
  other arithmetic: 71.9 us -> 0 us
  Pallas kernels: 0 us -> 61 us
  between operations: 14 us -> 0.64 us
  local copies, waits for them, and re-layouts: 10.7 us -> 0 us
  matrix products: 10.5 us -> 0 us
    psum x2 -> x0, blocking collectives: 566 us -> none  [prefix_states(): group_sum = lax.psum(local_state, 'shard')]
    all_gather x4 -> x0, waiting for transfers between devices: 242 us -> none  [entering(): gathered = lax.all_gather(array.astype(jnp.bfloat16), axis)]
    add x66 -> x0, other arithmetic: 70.6 us -> none  [add_states(): return earlier + later_part]
    pallas_call x0 -> x2, Pallas kernels: none -> 61 us  [the longest x1 57.4 us: body(): pl.pallas_call(functools.partial(scan_kernel, ny, nz), out_shape=(rows, r...]
    dot_general x12 -> x0, matrix products: 10.5 us -> none  [the longest x1 1.74 us: body(): jnp.einsum('shd,hde->she', key_heads, later_rounded, preferred_element_ty...]
  transfers between devices with their start and end apart: 4 -> 0, of which waited for: 4 -> 0; matrix products, arithmetic and copies ran while one was open for 2% -> 0% of each run, Pallas kernels for 0% -> 0%
where the time goes in v1:
time: 61.8 us; the launch traced here: 61.6 us
  Pallas kernels  61 us (99%)
  between operations  0.64 us (1%)
    pallas_call x1, Pallas kernels, body(): pl.pallas_call(functools.partial(scan_kernel, ny, nz), out_shape=(rows, r...  57.4 us
    pallas_call x1, Pallas kernels, body(): pl.pallas_call(final_kernel, grid=(2,), out_shape=(rows,) * 4, in_specs=[...  3.63 us

profile of v1, /device:TPU:1, one launch (start us, length us, event | category | flops | bytes accessed | tf_op | source)
XLA Modules:
  0.0 61.6 jit_solution(8370314001342039064)
XLA Ops:
  0.6 57.4 %scan.1 = (bf16[256,1024]{1,0:T(8,128)(2,1)}, bf16[256,1024]{1,0:T(8,128)(2,1)}, f32[256,1024]{1,0:T(8,128)}, f32[256,1024]{1,0:T(8,128)}, bf16[8,128,128]{2,1,0:T(8,128)(2,1)}) custom-call(bf16[256,1024]{1,0:T(8,128)(2,1)} %q_ref.1, bf16[256,1024]{1,0:T(8,128)(2,1)} %k_ref.3, bf16[256,1024]{1,0:T(8,128)(2,1)} %v_ref.3, bf16[256,1024]{1,0:T(8,128)(2,1)} %g_ref.1), custom_call_target="tpu_custom_call" | custom-call | tf_op jit(solution)/shard_map/scan/pallas_call | solution.py:193
  58.0 3.6 %final.1 = (bf16[256,1024]{1,0:T(8,128)(2,1)}, bf16[256,1024]{1,0:T(8,128)(2,1)}, bf16[256,1024]{1,0:T(8,128)(2,1)}, bf16[256,1024]{1,0:T(8,128)(2,1)}) custom-call(bf16[256,1024]{1,0:T(8,128)(2,1)} %k_ref.3, bf16[256,1024]{1,0:T(8,128)(2,1)} %v_ref.3, bf16[8,128,128]{2,1,0:T(8,128)(2,1)} %get-tuple-element.9.later_ref, ...), custom_call_target="tpu_custom_call" | custom-call | tf_op jit(solution)/shard_map/final/pallas_call | solution.py:212
